TPU v7x, 256 devices: a whole 4x4x8 slice. The times are simulated.
256 devices in a mesh: tm: 64 (over y_hi, x, z), rows: 4 (over y_lo, core).
Axes of the slice: x: 4, y: 4 (y_hi: 2, y_lo: 2; y = y_hi * 2 + y_lo), z: 8, core: 2. Of those that a mesh axis runs over, the one named last changes fastest.
Arguments:
- frames: bfloat16 [64, 32, 32, 640], P('tm', 'rows'), may hold values from -24 to 24
- conv_weight: bfloat16 [3, 3, 640, 640], replicated, may hold values from -0.078125 to 0.078125
- conv_bias: float32 [640], replicated, may hold values from -1.5 to 1.5
- ref_features: bfloat16 [1024, 640], P('tm'), may hold values from -6 to 6
- w_query: bfloat16 [640, 640], replicated, may hold values from -0.25 to 0.25
- w_key: bfloat16 [640, 640], replicated, may hold values from -0.25 to 0.25
- w_value: bfloat16 [640, 640], replicated, may hold values from -0.25 to 0.25
- w_out: bfloat16 [640, 640], replicated, may hold values from -0.25 to 0.25
- out_bias: float32 [640], replicated, may hold values from -1.5 to 1.5
Outputs:
- hidden: bfloat16 [64, 32, 32, 640], P('tm', 'rows')
- attended: bfloat16 [64, 32, 32, 640], P('tm', 'rows')
All inputs are finite; a program needn't handle non-finite values.
Results may differ from a plain program's by a relative error of at most 0.025.
Values may be sent and summed in bfloat16 or wider, within the bound.
A program may use at most 128 MiB of HBM per device.

v0:
```python
import jax
import jax.numpy as jnp
from jax import lax
from jax.sharding import PartitionSpec as P

HD = 80
key_block = 1024


def extended(value, sides, width):
    for axis, dim in sides:
        size, length = (lax.axis_size(axis), value.shape[dim])
        up = [(i, (i + 1) % size) for i in range(size - 1)]
        down = [(j, i) for i, j in up]
        last = lax.slice_in_dim(value, length - width, length, axis=dim)
        initial = lax.slice_in_dim(value, 0, width, axis=dim)
        before = lax.ppermute(last, axis, up)
        after = lax.ppermute(initial, axis, down)
        value = jnp.concatenate([before, value, after], axis=dim)
    return value


def attend_update(carry, query_heads, keys, values, heads):
    top, total, summed = carry
    count, band = (query_heads.shape[0], query_heads.shape[1])
    length = keys.shape[1]
    summed = summed.reshape(count, band, heads, HD)
    width = min(key_block, length)
    key_part = keys.reshape(keys.shape[0], width, heads, HD)
    value_part = values.reshape(values.shape[0], width, heads, HD)
    scores = jnp.einsum(
        "fqhd,khd->fhqk", query_heads, key_part[0], preferred_element_type=jnp.float32
    )
    scores = scores * HD ** (-0.5)
    new_top = jnp.maximum(top, jnp.max(scores, axis=3))
    factor = jnp.exp(top - new_top)
    weights = jnp.exp(scores - new_top[..., None])
    total = total * factor + jnp.sum(weights, axis=3)
    product = jnp.einsum(
        "fhqk,khd->fqhd",
        weights.astype(jnp.bfloat16),
        value_part[0],
        preferred_element_type=jnp.float32,
    )
    summed = summed * jnp.transpose(factor, (0, 2, 1))[..., None] + product
    return (new_top, total, summed.reshape(count, band, heads * HD))


def project_pair(source, w_key, w_value, count, channels):
    key = (
        jnp.dot(source, w_key, preferred_element_type=jnp.float32)
        .astype(jnp.bfloat16)
        .reshape(count, -1, channels)
    )
    value = (
        jnp.dot(source, w_value, preferred_element_type=jnp.float32)
        .astype(jnp.bfloat16)
        .reshape(count, -1, channels)
    )
    return (key, value)


def shards(frames, conv_weight, conv_bias, ref_features, w_query, w_key, w_value, w_out, out_bias):
    count, band_rows, width, channels = frames.shape
    heads = channels // HD
    band = band_rows * width
    activated = jax.nn.silu(frames.astype(jnp.float32)).astype(jnp.bfloat16)
    padded = extended(activated, (("rows", 1),), 1)
    padded = jnp.pad(padded, ((0, 0), (0, 0), (1, 1), (0, 0)))
    convolved = jnp.zeros((count * band, channels), jnp.float32)
    for row_tap in range(3):
        for col_tap in range(3):
            window = padded[:, row_tap : row_tap + band_rows, col_tap : col_tap + width].reshape(
                count * band, channels
            )
            convolved = convolved + jnp.dot(
                window, conv_weight[row_tap, col_tap], preferred_element_type=jnp.float32
            )
    hidden = (
        frames.reshape(count * band, channels).astype(jnp.float32) + convolved + conv_bias
    ).astype(jnp.bfloat16)
    query = jnp.dot(hidden, w_query, preferred_element_type=jnp.float32).astype(jnp.bfloat16)
    query_heads = query.reshape(count, band, heads, HD)
    start_state = (
        jnp.full((count, heads, band), -1e30, jnp.float32),
        jnp.zeros((count, heads, band), jnp.float32),
        jnp.zeros((count, band, channels), jnp.float32),
    )
    key, value = project_pair(hidden, w_key, w_value, count, channels)
    all_keys, all_values = (
        lax.all_gather(key, "rows", axis=1, tiled=True),
        lax.all_gather(value, "rows", axis=1, tiled=True),
    )
    state = attend_update(start_state, query_heads, all_keys, all_values, heads)
    ref_key = jnp.dot(ref_features, w_key, preferred_element_type=jnp.float32).astype(jnp.bfloat16)
    ref_value = jnp.dot(ref_features, w_value, preferred_element_type=jnp.float32).astype(
        jnp.bfloat16
    )
    every_key, every_value = (
        lax.all_gather(ref_key, "tm", axis=0, tiled=True),
        lax.all_gather(ref_value, "tm", axis=0, tiled=True),
    )
    state = attend_update(state, query_heads, every_key[None], every_value[None], heads)
    top, total, summed = state
    mixed = summed.reshape(count, band, heads, HD) / jnp.transpose(total, (0, 2, 1))[..., None]
    mixed = mixed.reshape(count * band, channels).astype(jnp.bfloat16)
    attended = (jnp.dot(mixed, w_out, preferred_element_type=jnp.float32) + out_bias).astype(
        jnp.bfloat16
    )
    return (
        hidden.reshape(count, band_rows, width, channels),
        attended.reshape(count, band_rows, width, channels),
    )


def solution(mesh):
    return jax.shard_map(
        shards,
        mesh=mesh,
        in_specs=(P("tm", "rows", None, None), P(), P(), P("tm", None), P(), P(), P(), P(), P()),
        out_specs=(P("tm", "rows", None, None), P("tm", "rows", None, None)),
        check_vma=False,
    )
```

profile of v0, /device:TPU:2, one launch (start us, length us, event | category | flops | bytes accessed | tf_op | source)
XLA Modules:
  0.0 329.9 jit_solution(8142130882859470929)
XLA Ops:
  7.2 1.3 multiply_convert_fusion
  8.6 2.0 collective-permute-start
  10.6 1.3 collective-permute-start.1
  11.9 3.2 collective-permute-done.1
  15.4 1.6 fusion.52
  17.1 0.5 fusion.43
  17.6 0.5 convolution_add_fusion.7
  18.1 0.5 convolution_add_fusion.6
  18.6 0.5 convolution_add_fusion.5
  19.1 0.5 convolution_add_fusion.4
  19.5 0.5 convolution_add_fusion.3
  20.0 0.5 convolution_add_fusion.2
  20.5 0.5 fusion.35
  21.0 1.2 convolution_convert_fusion.2
  22.2 1.2 convolution_convert_fusion
  23.5 0.8 convolution_convert_fusion.4
  24.6 0.8 convolution_convert_fusion.3
  26.1 26.4 %all-gather.11.cloned.1.call-done = bf16[1024,640]{1,0:T(8,128)(2,1)} async-done(((bf16[256,640]{1,0:T(8,128)(2,1)}), bf16[1024,640]{1,0:T(8,128)(2,1)}) %all-gather.11.cloned.1.call-update) | async-done | bytes 1310736 | tf_op jit(solution)/shard_map/all_gather | solution.py:91
  52.5 1.6 copy.19
  54.1 4.6 %bitcast_reduce_fusion.1 = (f32[8,256]{1,0:T(8,128)S(1)}, f32[8,1024,256]{2,1,0:T(8,128)}) fusion(bf16[1024,8,80]{0,2,1:T(8,128)(2,1)S(1)} %bitcast.200, bf16[256,8,80]{0,2,1:T(8,128)(2,1)S(1)} %bitcast.201), kind=kOutput, calls=%fused_computation.4 | convolution fusion | flops 339736576 | bytes 10035200 | tf_op jit(solution)/shard_map/fqhd,khd->fhqk/dot_general | solution.py:31
  58.7 22.4 %all-gather.13.cloned.1.call-done = bf16[1024,640]{1,0:T(8,128)(2,1)} async-done(((bf16[256,640]{1,0:T(8,128)(2,1)}), bf16[1024,640]{1,0:T(8,128)(2,1)}) %all-gather.13.cloned.1.call-update) | async-done | bytes 1310736 | tf_op jit(solution)/shard_map/all_gather | solution.py:92
  81.1 1.6 copy.21
  82.7 118.1 %all-gather.7.cloned.1.call-done = bf16[1024,640]{1,0:T(8,128)(2,1)} async-done(((bf16[16,640]{1,0:T(8,128)(2,1)}), bf16[1024,640]{1,0:T(8,128)(2,1)}) %all-gather.7.cloned.1.call-update) | async-done | bytes 1310736 | tf_op jit(solution)/shard_map/all_gather | solution.py:100
  200.9 1.6 copy.23
  202.5 2.4 bitcast_reduce_fusion
  204.9 1.1 copy-done.1
  206.0 2.7 fusion.2
  208.8 1.6 fusion.31
  210.4 105.2 %all-gather.9.cloned.1.call-done = bf16[1024,640]{1,0:T(8,128)(2,1)} async-done(((bf16[16,640]{1,0:T(8,128)(2,1)}), bf16[1024,640]{1,0:T(8,128)(2,1)}) %all-gather.9.cloned.1.call-update) | async-done | bytes 1310736 | tf_op jit(solution)/shard_map/all_gather | solution.py:101
  315.6 1.6 copy.24
  317.2 5.0 %fusion.40 = bf16[1,256,8,80]{1,3,2,0:T(8,128)(2,1)S(1)} fusion(f32[1,256,8,80]{1,3,2,0:T(8,128)S(1)} %fusion.31, bf16[1024,8,80]{0,2,1:T(8,128)(2,1)S(1)} %bitcast.206, f32[8,1024,256]{2,1,0:T(8,128)} %copy-done.2, f32[8,256]{1,0:T(8,128)S(1)} %get-tuple-element.15, f32[256,8]{0,1:T(8,128)S(1)} %get-tuple-element.12), kind=kOutput, calls=%fused_computation.45 | convolution fusion | flops 342327296 | bytes 10698752 | tf_op jit(solution)/shard_map/fhqk,khd->fqhd/dot_general | solution.py:39
  322.2 1.2 fusion.34
  (42 shorter events, 1.6 us)
Async XLA Ops:
  7.2 13.8 %copy-start = (bf16[640,640]{1,0:T(8,128)(2,1)S(1)}, bf16[640,640]{1,0:T(8,128)(2,1)}, u32[]{:S(2)}) copy-start(bf16[640,640]{1,0:T(8,128)(2,1)} %param.14) | copy-start | bytes 2457604
  7.2 45.3 %all-gather.11.cloned.1.call-start = ((), (), s32[]{:S(2)}) async-start(), calls=%async_computation.2 | async-start | bytes 1638400 | tf_op jit(solution)/shard_map/all_gather | solution.py:91
  7.2 9.8 %copy-start.3 = (bf16[3,3,640,640]{3,2,1,0:T(8,128)(2,1)S(1)}, bf16[3,3,640,640]{3,2,1,0:T(8,128)(2,1)}, u32[]{:S(2)}) copy-start(bf16[3,3,640,640]{3,2,1,0:T(8,128)(2,1)} %param.10) | copy-start | bytes 22118404
  8.6 3.3 %collective-permute-start = (bf16[1,1,32,640]{3,2,1,0:T(8,128)(2,1)S(1)}, bf16[1,1,32,640]{3,2,1,0:T(8,128)(2,1)S(1)}, u32[]{:S(2)}, u32[]{:S(2)}) collective-permute-start(bf16[1,1,32,640]{3,2,1,0:T(8,128)(2,1)S(1)} %get-tuple-element.10), channel_id=1, source_target_pairs={{0,1},{1,2},{2,3},{4,5},{5,6},{6,7},{8,9},{9,10},{10,11},{12,13},{... | collective-permute-start | bytes 122888 | tf_op jit(solution)/shard_map/ppermute | solution.py:17
  10.6 4.5 %collective-permute-start.1 = (bf16[1,1,32,640]{3,2,1,0:T(8,128)(2,1)S(1)}, bf16[1,1,32,640]{3,2,1,0:T(8,128)(2,1)S(1)}, u32[]{:S(2)}, u32[]{:S(2)}) collective-permute-start(bf16[1,1,32,640]{3,2,1,0:T(8,128)(2,1)S(1)} %get-tuple-element.11), channel_id=1, source_target_pairs={{1,0},{2,1},{3,2},{5,4},{6,5},{7,6},{9,8},{10,9},{11,10},{13,12},{... | collective-permute-start | bytes 122888 | tf_op jit(solution)/shard_map/ppermute | solution.py:18
  17.6 2.9 copy-start.7
  17.6 2.9 copy-start.10
  18.5 3.7 %copy-start.5 = (bf16[640,640]{1,0:T(8,128)(2,1)S(1)}, bf16[640,640]{1,0:T(8,128)(2,1)}, u32[]{:S(2)}) copy-start(bf16[640,640]{1,0:T(8,128)(2,1)} %param.15) | copy-start | bytes 2457604
  19.0 4.5 %copy-start.9 = (bf16[16,640]{1,0:T(8,128)(2,1)S(1)}, bf16[16,640]{1,0:T(8,128)(2,1)}, u32[]{:S(2)}) copy-start(bf16[16,640]{1,0:T(8,128)(2,1)} %param.12) | copy-start | bytes 61444
  19.0 6.4 %copy-start.8 = (bf16[640,640]{1,0:T(8,128)(2,1)S(1)}, bf16[640,640]{1,0:T(8,128)(2,1)}, u32[]{:S(2)}) copy-start(bf16[640,640]{1,0:T(8,128)(2,1)} %param.13) | copy-start | bytes 2457604
  21.0 37.7 %copy-start.4 = (bf16[256,640]{1,0:T(8,128)(2,1)}, bf16[256,640]{1,0:T(8,128)(2,1)S(1)}, u32[]{:S(2)}) copy-start(bf16[256,640]{1,0:T(8,128)(2,1)S(1)} %fusion.35) | copy-start | bytes 983044
  22.2 58.9 %all-gather.13.cloned.1.call-start = ((), (), s32[]{:S(2)}) async-start(), calls=%async_computation.3 | async-start | bytes 1638400 | tf_op jit(solution)/shard_map/all_gather | solution.py:92
  23.5 177.4 %all-gather.7.cloned.1.call-start = ((), (), s32[]{:S(2)}) async-start(), calls=%async_computation | async-start | bytes 1331200 | tf_op jit(solution)/shard_map/all_gather | solution.py:100
  24.4 291.2 %all-gather.9.cloned.1.call-start = ((), (), s32[]{:S(2)}) async-start(), calls=%async_computation.1 | async-start | bytes 1331200 | tf_op jit(solution)/shard_map/all_gather | solution.py:101
  26.1 56.6 %copy-start.6 = (bf16[256,640]{0,1:T(8,128)(2,1)}, bf16[256,640]{0,1:T(8,128)(2,1)S(1)}, u32[]{:S(2)}) copy-start(bf16[256,640]{0,1:T(8,128)(2,1)S(1)} %copy.20) | copy-start | bytes 983044
  202.5 3.6 %copy-start.1 = (f32[8,1024,256]{2,1,0:T(8,128)S(1)}, f32[8,1024,256]{2,1,0:T(8,128)}, u32[]{:S(2)}) copy-start(f32[8,1024,256]{2,1,0:T(8,128)} %get-tuple-element.20) | copy-start | bytes 25165828
  204.9 3.9 %copy-start.2 = (f32[8,1024,256]{2,1,0:T(8,128)}, f32[8,1024,256]{2,1,0:T(8,128)S(1)}, u32[]{:S(2)}) copy-start(f32[8,1024,256]{2,1,0:T(8,128)S(1)} %get-tuple-element.18) | copy-start | bytes 25165828
  210.4 111.8 %copy-start.12 = (f32[640]{0:T(1024)S(1)}, f32[640]{0:T(1024)}, u32[]{:S(2)}) copy-start(f32[640]{0:T(1024)} %param.17) | copy-start | bytes 7684
  317.2 5.0 %copy-start.11 = (bf16[640,640]{1,0:T(8,128)(2,1)S(1)}, bf16[640,640]{1,0:T(8,128)(2,1)}, u32[]{:S(2)}) copy-start(bf16[640,640]{1,0:T(8,128)(2,1)} %param.16) | copy-start | bytes 2457604
Sparse Core Ops, SparseCore 0:
  22.3 30.1 all-gather.10
  54.9 26.1 all-gather.12
  84.7 116.1 all-gather.6
  204.3 111.2 all-gather.8
where the time goes:
time: 330 us
  waiting for transfers between devices  275 us (83%)
  matrix products  24.5 us (7%)
  between operations  14.1 us (4%)
  local copies, waits for them, and re-layouts  7.96 us (2%)
  other arithmetic  4.31 us (1%)
  starting transfers between devices  3.64 us (1%)
    all_gather x1, waiting for transfers between devices, shards(): lax.all_gather(ref_key, 'tm', axis=0, tiled=True)  118 us
    all_gather x1, waiting for transfers between devices, shards(): lax.all_gather(ref_value, 'tm', axis=0, tiled=True)  105 us
    all_gather x1, waiting for transfers between devices, shards(): lax.all_gather(key, 'rows', axis=1, tiled=True)  26.4 us
    all_gather x1, waiting for transfers between devices, shards(): lax.all_gather(value, 'rows', axis=1, tiled=True)  22.4 us
    dot_general x2, matrix products, attend_update(): jnp.einsum('fqhd,khd->fhqk', query_heads, key_part[0], preferred_element_...  6.98 us
  transfers between devices with their start and end apart: 6, of which 5 were waited for; matrix products, arithmetic and copies ran while one was open for 6% of the time, Pallas kernels for 0%

commit v1 on v0

--- a/solution.py
+++ b/solution.py
@@ -87,10 +87,16 @@
         jnp.zeros((count, band, channels), jnp.float32),
     )
     key, value = project_pair(hidden, w_key, w_value, count, channels)
-    all_keys, all_values = (
-        lax.all_gather(key, "rows", axis=1, tiled=True),
-        lax.all_gather(value, "rows", axis=1, tiled=True),
-    )
+
+    def _order_wires(mat):
+        return jnp.concatenate(
+            lax.all_to_all(
+                jnp.stack([mat] * lax.axis_size("rows")), "rows", concat_axis=0, split_axis=0
+            ),
+            axis=1,
+        )
+
+    all_keys, all_values = (_order_wires(key), lax.all_gather(value, "rows", axis=1, tiled=True))
     state = attend_update(start_state, query_heads, all_keys, all_values, heads)
     ref_key = jnp.dot(ref_features, w_key, preferred_element_type=jnp.float32).astype(jnp.bfloat16)
     ref_value = jnp.dot(ref_features, w_value, preferred_element_type=jnp.float32).astype(

time: 330 us -> 308 us (0.933)
  waiting for transfers between devices: 275 us -> 246 us
  starting transfers between devices: 3.64 us -> 7.35 us
    all_gather x1 -> x0, waiting for transfers between devices: 26.4 us -> none  [shards(): lax.all_gather(key, 'rows', axis=1, tiled=True)]
    all_gather x1, waiting for transfers between devices: 22.4 us -> 0.01 us  [shards(): lax.all_gather(value, 'rows', axis=1, tiled=True)]
    all_to_all x0 -> x1, waiting for transfers between devices: none -> 18.4 us  [_order_wires(): lax.all_to_all(jnp.stack([mat] * lax.axis_size('rows')), 'rows', concat_a...]
    all_to_all x0 -> x1, starting transfers between devices: none -> 3.97 us  [_order_wires(): lax.all_to_all(jnp.stack([mat] * lax.axis_size('rows')), 'rows', concat_a...]
  transfers between devices with their start and end apart: 6 -> 6, of which waited for: 5 -> 4; matrix products, arithmetic and copies ran while one was open for 6% -> 8% of each run, Pallas kernels for 0% -> 0%
where the time goes in v1:
time: 308 us
  waiting for transfers between devices  246 us (80%)
  matrix products  25.9 us (8%)
  between operations  14.1 us (5%)
  local copies, waits for them, and re-layouts  10.4 us (3%)
  starting transfers between devices  7.35 us (2%)
  other arithmetic  4.31 us (1%)
    all_gather x1, waiting for transfers between devices, shards(): lax.all_gather(ref_key, 'tm', axis=0, tiled=True)  119 us
    all_gather x1, waiting for transfers between devices, shards(): lax.all_gather(ref_value, 'tm', axis=0, tiled=True)  105 us
    all_to_all x1, waiting for transfers between devices, _order_wires(): lax.all_to_all(jnp.stack([mat] * lax.axis_size('rows')), 'rows', concat_a...  18.4 us
    dot_general x2, matrix products, attend_update(): jnp.einsum('fqhd,khd->fhqk', query_heads, key_part[0], preferred_element_...  7.94 us
    dot_general x2, matrix products, attend_update(): jnp.einsum('fhqk,khd->fqhd', weights.astype(jnp.bfloat16), value_part[0],...  6.54 us
  transfers between devices with their start and end apart: 6, of which 4 were waited for; matrix products, arithmetic and copies ran while one was open for 8% of the time, Pallas kernels for 0%

profile of v1, /device:TPU:2, one launch (start us, length us, event | category | flops | bytes accessed | tf_op | source)
XLA Modules:
  0.0 307.6 jit_solution(5124590345611419357)
XLA Ops:
  7.2 1.3 multiply_convert_fusion
  8.6 2.0 collective-permute-start
  10.6 1.3 collective-permute-start.1
  11.9 3.2 %collective-permute-done.1 = bf16[1,1,32,640]{3,2,1,0:T(8,128)(2,1)S(1)} collective-permute-done((bf16[1,1,32,640]{3,2,1,0:T(8,128)(2,1)S(1)}, bf16[1,1,32,640]{3,2,1,0:T(8,128)(2,1)S(1)}, u32[]{:S(2)}, u32[]{:S(2)}) %collective-permute-start.1) | collective-permute-done | bytes 40992 | tf_op jit(solution)/shard_map/ppermute | solution.py:18
  15.4 1.6 fusion.52
  18.6 0.5 convolution_add_fusion.5
  19.0 0.5 convolution_add_fusion.4
  19.5 0.5 convolution_add_fusion.3
  20.0 0.5 convolution_add_fusion.2
  20.4 0.5 fusion.35
  20.9 1.2 convolution_convert_fusion
  22.2 0.9 convolution_convert_fusion.4
  23.7 1.1 stack.3
  24.9 4.0 %all-to-all-start = ((bf16[4,1,256,640]{2,3,1,0:T(8,128)(2,1)}), bf16[4,1,256,640]{2,3,1,0:T(8,128)(2,1)S(1)}, u32[]{:S(2)}, u32[]{:S(2)}) async-start(bf16[4,1,256,640]{2,3,1,0:T(8,128)(2,1)} %stack.3), calls=%async_computation | async-start | bytes 2621440 | tf_op jit(solution)/shard_map/all_to_all | solution.py:93
  28.9 0.8 convolution_convert_fusion.3
  29.7 1.6 convolution_convert_fusion.1
  31.3 0.9 copy.28
  32.3 18.4 %all-to-all-done = bf16[4,1,256,640]{2,3,1,0:T(8,128)(2,1)S(1)} async-done(((bf16[4,1,256,640]{2,3,1,0:T(8,128)(2,1)}), bf16[4,1,256,640]{2,3,1,0:T(8,128)(2,1)S(1)}, u32[]{:S(2)}, u32[]{:S(2)}) %all-to-all-start) | async-done | bytes 1310752 | tf_op jit(solution)/shard_map/all_to_all | solution.py:93
  50.7 1.0 copy.27
  51.7 1.0 squeeze_reshape_reshape.3
  52.6 5.5 %bitcast_reduce_fusion.1 = (f32[8,256]{1,0:T(8,128)S(1)}, f32[8,1024,256]{2,1,0:T(8,128)}) fusion(bf16[1024,8,80]{0,2,1:T(8,128)(2,1)S(1)} %squeeze_reshape_reshape.3, bf16[256,8,80]{0,2,1:T(8,128)(2,1)} %bitcast.201), kind=kOutput, calls=%fused_computation.4 | convolution fusion | flops 339736576 | bytes 10035200 | tf_op jit(solution)/shard_map/fqhd,khd->fhqk/dot_general | solution.py:31
  58.2 1.6 copy.29
  59.8 118.6 %all-gather.5.cloned.1.call-done = bf16[1024,640]{1,0:T(8,128)(2,1)} async-done(((bf16[16,640]{1,0:T(8,128)(2,1)}), bf16[1024,640]{1,0:T(8,128)(2,1)}) %all-gather.5.cloned.1.call-update) | async-done | bytes 1310736 | tf_op jit(solution)/shard_map/all_gather | solution.py:106
  178.4 1.6 copy.31
  180.0 2.4 bitcast_reduce_fusion
  182.5 1.1 copy-done.1
  183.5 2.7 fusion.2
  186.3 1.6 fusion.31
  187.9 105.4 %all-gather.7.cloned.1.call-done = bf16[1024,640]{1,0:T(8,128)(2,1)} async-done(((bf16[16,640]{1,0:T(8,128)(2,1)}), bf16[1024,640]{1,0:T(8,128)(2,1)}) %all-gather.7.cloned.1.call-update) | async-done | bytes 1310736 | tf_op jit(solution)/shard_map/all_gather | solution.py:107
  293.3 1.6 copy.32
  294.9 5.0 %fusion.40 = bf16[1,256,8,80]{1,3,2,0:T(8,128)(2,1)S(1)} fusion(f32[1,256,8,80]{1,3,2,0:T(8,128)S(1)} %fusion.31, bf16[1024,8,80]{0,2,1:T(8,128)(2,1)S(1)} %bitcast.206, f32[8,1024,256]{2,1,0:T(8,128)} %copy-done.2, f32[8,256]{1,0:T(8,128)S(1)} %get-tuple-element.15, f32[256,8]{0,1:T(8,128)S(1)} %get-tuple-element.12), kind=kOutput, calls=%fused_computation.45 | convolution fusion | flops 342327296 | bytes 10698752 | tf_op jit(solution)/shard_map/fhqk,khd->fqhd/dot_general | solution.py:39
  299.9 1.2 fusion.34
  (40 shorter events, 2.7 us)
Async XLA Ops:
  7.2 15.0 %copy-start = (bf16[640,640]{1,0:T(8,128)(2,1)S(1)}, bf16[640,640]{1,0:T(8,128)(2,1)}, u32[]{:S(2)}) copy-start(bf16[640,640]{1,0:T(8,128)(2,1)} %param.14) | copy-start | bytes 2457604
  7.2 51.0 %all-gather.9.cloned.1.call-start = ((), (), s32[]{:S(2)}) async-start(), calls=%async_computation.3 | async-start | bytes 1638400 | tf_op jit(solution)/shard_map/all_gather | solution.py:99
  7.2 9.8 %copy-start.3 = (bf16[3,3,640,640]{3,2,1,0:T(8,128)(2,1)S(1)}, bf16[3,3,640,640]{3,2,1,0:T(8,128)(2,1)}, u32[]{:S(2)}) copy-start(bf16[3,3,640,640]{3,2,1,0:T(8,128)(2,1)} %param.10) | copy-start | bytes 22118404
  8.6 3.3 %collective-permute-start = (bf16[1,1,32,640]{3,2,1,0:T(8,128)(2,1)S(1)}, bf16[1,1,32,640]{3,2,1,0:T(8,128)(2,1)S(1)}, u32[]{:S(2)}, u32[]{:S(2)}) collective-permute-start(bf16[1,1,32,640]{3,2,1,0:T(8,128)(2,1)S(1)} %get-tuple-element.10), channel_id=1, source_target_pairs={{0,1},{1,2},{2,3},{4,5},{5,6},{6,7},{8,9},{9,10},{10,11},{12,13},{... | collective-permute-start | bytes 122888 | tf_op jit(solution)/shard_map/ppermute | solution.py:17
  10.6 4.5 %collective-permute-start.1 = (bf16[1,1,32,640]{3,2,1,0:T(8,128)(2,1)S(1)}, bf16[1,1,32,640]{3,2,1,0:T(8,128)(2,1)S(1)}, u32[]{:S(2)}, u32[]{:S(2)}) collective-permute-start(bf16[1,1,32,640]{3,2,1,0:T(8,128)(2,1)S(1)} %get-tuple-element.11), channel_id=1, source_target_pairs={{1,0},{2,1},{3,2},{5,4},{6,5},{7,6},{9,8},{10,9},{11,10},{13,12},{... | collective-permute-start | bytes 122888 | tf_op jit(solution)/shard_map/ppermute | solution.py:18
  17.6 2.8 copy-start.6
  17.6 2.8 copy-start.8
  18.1 2.8 copy-start.5
  18.5 3.7 %copy-start.7 = (bf16[16,640]{1,0:T(8,128)(2,1)S(1)}, bf16[16,640]{1,0:T(8,128)(2,1)}, u32[]{:S(2)}) copy-start(bf16[16,640]{1,0:T(8,128)(2,1)} %param.12) | copy-start | bytes 61444
  20.9 11.3 %copy-start.4 = (bf16[256,640]{1,0:T(8,128)(2,1)}, bf16[256,640]{1,0:T(8,128)(2,1)S(1)}, u32[]{:S(2)}) copy-start(bf16[256,640]{1,0:T(8,128)(2,1)S(1)} %fusion.35) | copy-start | bytes 983044
  22.1 156.2 %all-gather.5.cloned.1.call-start = ((), (), s32[]{:S(2)}) async-start(), calls=%async_computation.1 | async-start | bytes 1331200 | tf_op jit(solution)/shard_map/all_gather | solution.py:106
  24.9 25.8 %all-to-all-start = ((bf16[4,1,256,640]{2,3,1,0:T(8,128)(2,1)}), bf16[4,1,256,640]{2,3,1,0:T(8,128)(2,1)S(1)}, u32[]{:S(2)}, u32[]{:S(2)}) async-start(bf16[4,1,256,640]{2,3,1,0:T(8,128)(2,1)} %stack.3), calls=%async_computation | async-start | bytes 2621440 | tf_op jit(solution)/shard_map/all_to_all | solution.py:93
  28.9 264.4 %all-gather.7.cloned.1.call-start = ((), (), s32[]{:S(2)}) async-start(), calls=%async_computation.2 | async-start | bytes 1331200 | tf_op jit(solution)/shard_map/all_gather | solution.py:107
  180.0 3.6 %copy-start.1 = (f32[8,1024,256]{2,1,0:T(8,128)S(1)}, f32[8,1024,256]{2,1,0:T(8,128)}, u32[]{:S(2)}) copy-start(f32[8,1024,256]{2,1,0:T(8,128)} %get-tuple-element.20) | copy-start | bytes 25165828
  182.4 3.9 %copy-start.2 = (f32[8,1024,256]{2,1,0:T(8,128)}, f32[8,1024,256]{2,1,0:T(8,128)S(1)}, u32[]{:S(2)}) copy-start(f32[8,1024,256]{2,1,0:T(8,128)S(1)} %get-tuple-element.18) | copy-start | bytes 25165828
  187.9 112.0 %copy-start.10 = (f32[640]{0:T(1024)S(1)}, f32[640]{0:T(1024)}, u32[]{:S(2)}) copy-start(f32[640]{0:T(1024)} %param.17) | copy-start | bytes 7684
  294.9 5.0 %copy-start.9 = (bf16[640,640]{1,0:T(8,128)(2,1)S(1)}, bf16[640,640]{1,0:T(8,128)(2,1)}, u32[]{:S(2)}) copy-start(bf16[640,640]{1,0:T(8,128)(2,1)} %param.16) | copy-start | bytes 2457604
Sparse Core Ops, SparseCore 0:
  22.3 34.6 all-gather.8
  60.6 117.7 all-gather.4
  182.0 111.2 all-gather.6
